TPU v7x, 32 devices: a whole 2x2x4 slice. The times are simulated.
32 devices in a mesh: vel: 4 (over y, x), space: 8 (over z, core).
Axes of the slice: x: 2, y: 2, z: 4, core: 2. Of those that a mesh axis runs over, the one named last changes fastest.
Arguments:
- density: float32 [1024, 32, 8, 128], P('vel', 'space'), may hold values from -6 to 6
- limiter: int32 [32, 8, 128], P('space'), may hold values from 0 to 2
- heading: int32 [1024], P('vel'), may hold values from 0 to 1
- courant: float32 [1024], P('vel'), may hold values from 0.1 to 0.9
- kernel_slices: bfloat16 [16, 1024, 1024], P('space', None, 'vel'), may hold values from -0.046875 to 0.046875
Outputs:
- transported: float32 [1024, 32, 8, 128], P('vel', 'space')
- collision: float32 [1024, 32, 8, 128], P('vel', 'space')
Inputs may be any that keep to these rules, and one draw needn't show every extreme that they name: `limiter`: 0 no slope, 1 minmod slope, 2 central slope.
All inputs are finite; a program needn't handle non-finite values.
Results may differ from a plain program's by a relative error of at most 0.0041.
Values may be sent and summed in bfloat16 or wider, within the bound.
A program may use at most 128 MiB of HBM per device.

v0:
```python
import jax
import jax.numpy as jnp
from jax import lax
from jax.sharding import PartitionSpec as P

V = 1024
SLICES = 16


def extended(shard, sides, width):
    for axis, dim in sides:
        size, length = (lax.axis_size(axis), shard.shape[dim])
        up = [(i, (i + 1) % size) for i in range(size - 1)]
        down = [(j, i) for i, j in up]
        last = lax.slice_in_dim(shard, length - width, length, axis=dim)
        first = lax.slice_in_dim(shard, 0, width, axis=dim)
        before = lax.ppermute(last, axis, up)
        after = lax.ppermute(first, axis, down)
        shard = jnp.concatenate([before, shard, after], axis=dim)
    return shard


def limited_slopes(left_diff, right_diff, limiter):
    minmod_slope = jnp.where(
        left_diff * right_diff > 0,
        jnp.sign(left_diff) * jnp.minimum(jnp.abs(left_diff), jnp.abs(right_diff)),
        jnp.zeros_like(left_diff),
    )
    central = 0.5 * (left_diff + right_diff)
    codes = limiter[None]
    return jnp.where(
        codes == 1, minmod_slope, jnp.where(codes == 2, central, jnp.zeros_like(central))
    )


def make_fold(source, totals, pieces):
    stride = V // SLICES

    def one_slice(counter, running):
        matrix = lax.dynamic_index_in_dim(pieces, counter, 0, keepdims=False)
        projected = lax.dot_general(
            matrix, source, (((0,), (0,)), ((), ())), preferred_element_type=jnp.float32
        )
        weight = lax.dynamic_index_in_dim(source, counter * stride, 0, keepdims=True).astype(
            jnp.float32
        )
        return running + weight * projected

    return lax.fori_loop(0, pieces.shape[0], one_slice, totals)


def local(density, limiter, heading, courant, kernel_slices):
    padded = extended(density, (("space", 1),), 1)
    left_diff = density - padded[:, :-2]
    right_diff = padded[:, 2:] - density
    slopes = limited_slopes(left_diff, right_diff, limiter)
    upwind = (2 * heading - 1).astype(jnp.float32)[:, None, None, None]
    rebuilt = density + 0.5 * upwind * slopes
    rebuilt_pad = extended(rebuilt, (("space", 1),), 1)
    forward = (heading == 1)[:, None, None, None]
    upstream = jnp.where(forward, rebuilt_pad[:, :-2], rebuilt_pad[:, 2:])
    transported = density - courant[:, None, None, None] * (rebuilt - upstream)
    flattened = transported.astype(jnp.bfloat16).reshape(density.shape[0], -1)
    everyone = lax.all_gather(flattened, "vel", axis=0, tiled=True)
    initial = jnp.zeros(flattened.shape, jnp.float32)
    restored = make_fold(
        everyone, initial, lax.all_gather(kernel_slices, "space", axis=0, tiled=True)
    )
    return (transported, restored.reshape(density.shape))


def solution(mesh):
    return jax.shard_map(
        local,
        mesh=mesh,
        in_specs=(
            P("vel", "space", None, None),
            P("space", None, None),
            P("vel"),
            P("vel"),
            P("space", None, "vel"),
        ),
        out_specs=(P("vel", "space", None, None), P("vel", "space", None, None)),
        check_vma=False,
    )
```

profile of v0, /device:TPU:0, one launch (start us, length us, event | category | flops | bytes accessed | tf_op | source)
XLA Modules:
  0.0 402.4 jit_solution(9619417374742082083)
XLA Ops:
  7.2 1.8 fusion.16
  9.1 2.6 collective-permute-start
  11.7 1.3 collective-permute-start.1
  13.0 0.9 collective-permute-done
  13.9 4.5 %collective-permute-done.1 = f32[256,1,8,128]{3,2,1,0:T(8,128)S(1)} collective-permute-done((f32[256,1,8,128]{3,2,1,0:T(8,128)S(1)}, f32[256,1,8,128]{3,2,1,0:T(8,128)S(1)}, u32[]{:S(2)}, u32[]{:S(2)}) %collective-permute-start.1) | collective-permute-done | bytes 1048608 | tf_op jit(solution)/shard_map/ppermute | solution.py:18
  18.4 3.6 multiply_add_fusion
  22.1 14.0 %collective-permute-start.2 = (f32[256,1,8,128]{3,2,1,0:T(8,128)S(1)}, f32[256,1,8,128]{3,2,1,0:T(8,128)S(1)}, u32[]{:S(2)}, u32[]{:S(2)}) collective-permute-start(f32[256,1,8,128]{3,2,1,0:T(8,128)S(1)} %get-tuple-element.107), channel_id=1, source_target_pairs={{0,1},{1,2},{2,3},{3,4},{4,5},{5,6},{6,7},{8,9},{9,10},{10,11},{11... | collective-permute-start | bytes 3145736 | tf_op jit(solution)/shard_map/ppermute | solution.py:17
  36.1 1.3 collective-permute-start.3
  37.4 0.9 collective-permute-done.2
  38.3 2.4 collective-permute-done.3
  40.7 4.1 %fusion.13 = (bf16[256,4,8,128]{3,2,1,0:T(8,128)(2,1)S(1)}, f32[256,4,8,128]{3,2,1,0:T(8,128)}) fusion(f32[256,4,8,128]{3,2,1,0:T(8,128)S(1)} %copy-done, f32[256,4,8,128]{3,2,1,0:T(8,128)S(1)} %multiply_add_fusion, f32[256,1,8,128]{3,2,1,0:T(8,128)S(1)} %collective-permute-done.3, f32[256,1,8,128]{3,2,1,0:T(8,128)S(1)} %collective-permute-done.2, ...), kind=kLoop, calls=%fused_computation.25 | loop fusion | flops 7340032 | bytes 16778496 | tf_op jit(solution)/shard_map/convert_element_type | solution.py:63
  44.8 2.3 copy.10
  47.9 98.3 %all-gather.3.cloned.1.call-done = bf16[1024,4096]{1,0:T(8,128)(2,1)} async-done(((bf16[256,4096]{1,0:T(8,128)(2,1)}), bf16[1024,4096]{1,0:T(8,128)(2,1)}) %all-gather.3.cloned.1.call-update) | async-done | bytes 8388624 | tf_op jit(solution)/shard_map/all_gather | solution.py:64
  146.2 83.7 %all-gather.5.cloned.1.call-done = bf16[16,1024,256]{2,1,0:T(8,128)(2,1)} async-done(((bf16[2,1024,256]{2,1,0:T(8,128)(2,1)}), bf16[16,1024,256]{2,1,0:T(8,128)(2,1)}) %all-gather.5.cloned.1.call-update) | async-done | bytes 8388624 | tf_op jit(solution)/shard_map/all_gather | solution.py:67
  229.8 160.8 %while.14 = (s32[]{:T(128)}, f32[256,4096]{1,0:T(8,128)}, bf16[1024,4096]{1,0:T(8,128)(2,1)}, bf16[16,1024,256]{2,1,0:T(8,128)(2,1)}, s32[]{:T(128)}, /*index=5*/s32[]{:T(128)}, s32[]{:T(128)}, s32[]{:T(128)}) while((s32[]{:T(128)}, f32[256,4096]{1,0:T(8,128)}, bf16[1024,4096]{1,0:T(8,128)(2,1)}, bf16[16,1024,256]{2,1,0:T(8,128)(2,1)}, ...), condition=%wide.region_1.2_spmd.clone, body=%wide.region_0.1_spmd.clone.sunk | while | flops 2150633472 | bytes 17343120 | solution.py:49
  230.7 8.1 %fusion.23 = f32[256,4096]{1,0:T(8,128)} fusion(bf16[1024,4096]{1,0:T(8,128)(2,1)} %get-tuple-element.156, f32[256,4096]{1,0:T(8,128)} %get-tuple-element.147, f32[4096]{0:T(1024)S(1)} %bitcast.23, pred[]{:T(512)S(6)} %compare.3, bf16[16,1024,256]{2,1,0:T(8,128)(2,1)} %get-tuple-element.157, s32[]{:T(128)} %get-tuple-element.146), kind=kOutput, calls=%fused_computation.1.clone.1 | convolution fusion | flops 2150629376 | bytes 17318400 | tf_op jit(solution)/shard_map/while/body/eval_jaxpr/dot_general | solution.py:41
  239.6 9.3 %fusion.23 = f32[256,4096]{1,0:T(8,128)} fusion(bf16[1024,4096]{1,0:T(8,128)(2,1)} %get-tuple-element.156, f32[256,4096]{1,0:T(8,128)} %get-tuple-element.147, f32[4096]{0:T(1024)S(1)} %bitcast.23, pred[]{:T(512)S(6)} %compare.3, bf16[16,1024,256]{2,1,0:T(8,128)(2,1)} %get-tuple-element.157, s32[]{:T(128)} %get-tuple-element.146), kind=kOutput, calls=%fused_computation.1.clone.1 | convolution fusion | flops 2150629376 | bytes 17318400 | tf_op jit(solution)/shard_map/while/body/eval_jaxpr/dot_general | solution.py:41
  249.7 9.3 %fusion.23 = f32[256,4096]{1,0:T(8,128)} fusion(bf16[1024,4096]{1,0:T(8,128)(2,1)} %get-tuple-element.156, f32[256,4096]{1,0:T(8,128)} %get-tuple-element.147, f32[4096]{0:T(1024)S(1)} %bitcast.23, pred[]{:T(512)S(6)} %compare.3, bf16[16,1024,256]{2,1,0:T(8,128)(2,1)} %get-tuple-element.157, s32[]{:T(128)} %get-tuple-element.146), kind=kOutput, calls=%fused_computation.1.clone.1 | convolution fusion | flops 2150629376 | bytes 17318400 | tf_op jit(solution)/shard_map/while/body/eval_jaxpr/dot_general | solution.py:41
  259.9 9.3 %fusion.23 = f32[256,4096]{1,0:T(8,128)} fusion(bf16[1024,4096]{1,0:T(8,128)(2,1)} %get-tuple-element.156, f32[256,4096]{1,0:T(8,128)} %get-tuple-element.147, f32[4096]{0:T(1024)S(1)} %bitcast.23, pred[]{:T(512)S(6)} %compare.3, bf16[16,1024,256]{2,1,0:T(8,128)(2,1)} %get-tuple-element.157, s32[]{:T(128)} %get-tuple-element.146), kind=kOutput, calls=%fused_computation.1.clone.1 | convolution fusion | flops 2150629376 | bytes 17318400 | tf_op jit(solution)/shard_map/while/body/eval_jaxpr/dot_general | solution.py:41
  270.0 9.3 %fusion.23 = f32[256,4096]{1,0:T(8,128)} fusion(bf16[1024,4096]{1,0:T(8,128)(2,1)} %get-tuple-element.156, f32[256,4096]{1,0:T(8,128)} %get-tuple-element.147, f32[4096]{0:T(1024)S(1)} %bitcast.23, pred[]{:T(512)S(6)} %compare.3, bf16[16,1024,256]{2,1,0:T(8,128)(2,1)} %get-tuple-element.157, s32[]{:T(128)} %get-tuple-element.146), kind=kOutput, calls=%fused_computation.1.clone.1 | convolution fusion | flops 2150629376 | bytes 17318400 | tf_op jit(solution)/shard_map/while/body/eval_jaxpr/dot_general | solution.py:41
  280.1 9.3 %fusion.23 = f32[256,4096]{1,0:T(8,128)} fusion(bf16[1024,4096]{1,0:T(8,128)(2,1)} %get-tuple-element.156, f32[256,4096]{1,0:T(8,128)} %get-tuple-element.147, f32[4096]{0:T(1024)S(1)} %bitcast.23, pred[]{:T(512)S(6)} %compare.3, bf16[16,1024,256]{2,1,0:T(8,128)(2,1)} %get-tuple-element.157, s32[]{:T(128)} %get-tuple-element.146), kind=kOutput, calls=%fused_computation.1.clone.1 | convolution fusion | flops 2150629376 | bytes 17318400 | tf_op jit(solution)/shard_map/while/body/eval_jaxpr/dot_general | solution.py:41
  290.2 9.3 %fusion.23 = f32[256,4096]{1,0:T(8,128)} fusion(bf16[1024,4096]{1,0:T(8,128)(2,1)} %get-tuple-element.156, f32[256,4096]{1,0:T(8,128)} %get-tuple-element.147, f32[4096]{0:T(1024)S(1)} %bitcast.23, pred[]{:T(512)S(6)} %compare.3, bf16[16,1024,256]{2,1,0:T(8,128)(2,1)} %get-tuple-element.157, s32[]{:T(128)} %get-tuple-element.146), kind=kOutput, calls=%fused_computation.1.clone.1 | convolution fusion | flops 2150629376 | bytes 17318400 | tf_op jit(solution)/shard_map/while/body/eval_jaxpr/dot_general | solution.py:41
  300.4 9.3 %fusion.23 = f32[256,4096]{1,0:T(8,128)} fusion(bf16[1024,4096]{1,0:T(8,128)(2,1)} %get-tuple-element.156, f32[256,4096]{1,0:T(8,128)} %get-tuple-element.147, f32[4096]{0:T(1024)S(1)} %bitcast.23, pred[]{:T(512)S(6)} %compare.3, bf16[16,1024,256]{2,1,0:T(8,128)(2,1)} %get-tuple-element.157, s32[]{:T(128)} %get-tuple-element.146), kind=kOutput, calls=%fused_computation.1.clone.1 | convolution fusion | flops 2150629376 | bytes 17318400 | tf_op jit(solution)/shard_map/while/body/eval_jaxpr/dot_general | solution.py:41
  310.5 9.3 %fusion.23 = f32[256,4096]{1,0:T(8,128)} fusion(bf16[1024,4096]{1,0:T(8,128)(2,1)} %get-tuple-element.156, f32[256,4096]{1,0:T(8,128)} %get-tuple-element.147, f32[4096]{0:T(1024)S(1)} %bitcast.23, pred[]{:T(512)S(6)} %compare.3, bf16[16,1024,256]{2,1,0:T(8,128)(2,1)} %get-tuple-element.157, s32[]{:T(128)} %get-tuple-element.146), kind=kOutput, calls=%fused_computation.1.clone.1 | convolution fusion | flops 2150629376 | bytes 17318400 | tf_op jit(solution)/shard_map/while/body/eval_jaxpr/dot_general | solution.py:41
  320.6 9.3 %fusion.23 = f32[256,4096]{1,0:T(8,128)} fusion(bf16[1024,4096]{1,0:T(8,128)(2,1)} %get-tuple-element.156, f32[256,4096]{1,0:T(8,128)} %get-tuple-element.147, f32[4096]{0:T(1024)S(1)} %bitcast.23, pred[]{:T(512)S(6)} %compare.3, bf16[16,1024,256]{2,1,0:T(8,128)(2,1)} %get-tuple-element.157, s32[]{:T(128)} %get-tuple-element.146), kind=kOutput, calls=%fused_computation.1.clone.1 | convolution fusion | flops 2150629376 | bytes 17318400 | tf_op jit(solution)/shard_map/while/body/eval_jaxpr/dot_general | solution.py:41
  330.7 9.3 %fusion.23 = f32[256,4096]{1,0:T(8,128)} fusion(bf16[1024,4096]{1,0:T(8,128)(2,1)} %get-tuple-element.156, f32[256,4096]{1,0:T(8,128)} %get-tuple-element.147, f32[4096]{0:T(1024)S(1)} %bitcast.23, pred[]{:T(512)S(6)} %compare.3, bf16[16,1024,256]{2,1,0:T(8,128)(2,1)} %get-tuple-element.157, s32[]{:T(128)} %get-tuple-element.146), kind=kOutput, calls=%fused_computation.1.clone.1 | convolution fusion | flops 2150629376 | bytes 17318400 | tf_op jit(solution)/shard_map/while/body/eval_jaxpr/dot_general | solution.py:41
  340.9 9.3 %fusion.23 = f32[256,4096]{1,0:T(8,128)} fusion(bf16[1024,4096]{1,0:T(8,128)(2,1)} %get-tuple-element.156, f32[256,4096]{1,0:T(8,128)} %get-tuple-element.147, f32[4096]{0:T(1024)S(1)} %bitcast.23, pred[]{:T(512)S(6)} %compare.3, bf16[16,1024,256]{2,1,0:T(8,128)(2,1)} %get-tuple-element.157, s32[]{:T(128)} %get-tuple-element.146), kind=kOutput, calls=%fused_computation.1.clone.1 | convolution fusion | flops 2150629376 | bytes 17318400 | tf_op jit(solution)/shard_map/while/body/eval_jaxpr/dot_general | solution.py:41
  351.0 9.3 %fusion.23 = f32[256,4096]{1,0:T(8,128)} fusion(bf16[1024,4096]{1,0:T(8,128)(2,1)} %get-tuple-element.156, f32[256,4096]{1,0:T(8,128)} %get-tuple-element.147, f32[4096]{0:T(1024)S(1)} %bitcast.23, pred[]{:T(512)S(6)} %compare.3, bf16[16,1024,256]{2,1,0:T(8,128)(2,1)} %get-tuple-element.157, s32[]{:T(128)} %get-tuple-element.146), kind=kOutput, calls=%fused_computation.1.clone.1 | convolution fusion | flops 2150629376 | bytes 17318400 | tf_op jit(solution)/shard_map/while/body/eval_jaxpr/dot_general | solution.py:41
  361.1 9.3 %fusion.23 = f32[256,4096]{1,0:T(8,128)} fusion(bf16[1024,4096]{1,0:T(8,128)(2,1)} %get-tuple-element.156, f32[256,4096]{1,0:T(8,128)} %get-tuple-element.147, f32[4096]{0:T(1024)S(1)} %bitcast.23, pred[]{:T(512)S(6)} %compare.3, bf16[16,1024,256]{2,1,0:T(8,128)(2,1)} %get-tuple-element.157, s32[]{:T(128)} %get-tuple-element.146), kind=kOutput, calls=%fused_computation.1.clone.1 | convolution fusion | flops 2150629376 | bytes 17318400 | tf_op jit(solution)/shard_map/while/body/eval_jaxpr/dot_general | solution.py:41
  371.2 9.3 %fusion.23 = f32[256,4096]{1,0:T(8,128)} fusion(bf16[1024,4096]{1,0:T(8,128)(2,1)} %get-tuple-element.156, f32[256,4096]{1,0:T(8,128)} %get-tuple-element.147, f32[4096]{0:T(1024)S(1)} %bitcast.23, pred[]{:T(512)S(6)} %compare.3, bf16[16,1024,256]{2,1,0:T(8,128)(2,1)} %get-tuple-element.157, s32[]{:T(128)} %get-tuple-element.146), kind=kOutput, calls=%fused_computation.1.clone.1 | convolution fusion | flops 2150629376 | bytes 17318400 | tf_op jit(solution)/shard_map/while/body/eval_jaxpr/dot_general | solution.py:41
  381.4 9.3 %fusion.23 = f32[256,4096]{1,0:T(8,128)} fusion(bf16[1024,4096]{1,0:T(8,128)(2,1)} %get-tuple-element.156, f32[256,4096]{1,0:T(8,128)} %get-tuple-element.147, f32[4096]{0:T(1024)S(1)} %bitcast.23, pred[]{:T(512)S(6)} %compare.3, bf16[16,1024,256]{2,1,0:T(8,128)(2,1)} %get-tuple-element.157, s32[]{:T(128)} %get-tuple-element.146), kind=kOutput, calls=%fused_computation.1.clone.1 | convolution fusion | flops 2150629376 | bytes 17318400 | tf_op jit(solution)/shard_map/while/body/eval_jaxpr/dot_general | solution.py:41
  390.6 5.0 %copy.8 = f32[32,8,32,128]{3,2,1,0:T(8,128)} copy(f32[32,8,32,128]{3,1,2,0:T(8,128)} %bitcast.19) | data formatting | bytes 8388608
  (33 shorter events, 14.6 us)
Async XLA Ops:
  7.2 5.8 %copy-start.3 = (s32[256]{0:T(256)S(1)}, s32[256]{0:T(256)}, u32[]{:S(2)}) copy-start(s32[256]{0:T(256)} %param.9) | copy-start | bytes 3076
  7.2 5.8 %copy-start.1 = (s32[4,8,128]{2,1,0:T(8,128)S(1)}, s32[4,8,128]{2,1,0:T(8,128)}, u32[]{:S(2)}) copy-start(s32[4,8,128]{2,1,0:T(8,128)} %param.8) | copy-start | bytes 49156
  7.2 139.0 %all-gather.3.cloned.1.call-start = ((), (), s32[]{:S(2)}) async-start(), calls=%async_computation | async-start | bytes 10485760 | tf_op jit(solution)/shard_map/all_gather | solution.py:64
  7.2 11.1 %copy-start = (f32[256,4,8,128]{3,2,1,0:T(8,128)S(1)}, f32[256,4,8,128]{3,2,1,0:T(8,128)}, u32[]{:S(2)}) copy-start(f32[256,4,8,128]{3,2,1,0:T(8,128)} %param.7) | copy-start | bytes 12582916
  9.1 4.8 %collective-permute-start = (f32[256,1,8,128]{3,2,1,0:T(8,128)S(1)}, f32[256,1,8,128]{3,2,1,0:T(8,128)S(1)}, u32[]{:S(2)}, u32[]{:S(2)}) collective-permute-start(f32[256,1,8,128]{3,2,1,0:T(8,128)S(1)} %get-tuple-element.109), channel_id=1, source_target_pairs={{0,1},{1,2},{2,3},{3,4},{4,5},{5,6},{6,7},{8,9},{9,10},{10,11},{11... | collective-permute-start | bytes 3145736 | tf_op jit(solution)/shard_map/ppermute | solution.py:17
  11.7 6.7 %collective-permute-start.1 = (f32[256,1,8,128]{3,2,1,0:T(8,128)S(1)}, f32[256,1,8,128]{3,2,1,0:T(8,128)S(1)}, u32[]{:S(2)}, u32[]{:S(2)}) collective-permute-start(f32[256,1,8,128]{3,2,1,0:T(8,128)S(1)} %get-tuple-element.110), channel_id=1, source_target_pairs={{1,0},{2,1},{3,2},{4,3},{5,4},{6,5},{7,6},{9,8},{10,9},{11,10},{12... | collective-permute-start | bytes 3145736 | tf_op jit(solution)/shard_map/ppermute | solution.py:18
  21.9 18.8 %copy-start.2 = (f32[256]{0:T(256)S(1)}, f32[256]{0:T(256)}, u32[]{:S(2)}) copy-start(f32[256]{0:T(256)} %param.10) | copy-start | bytes 3076
  22.1 16.2 %collective-permute-start.2 = (f32[256,1,8,128]{3,2,1,0:T(8,128)S(1)}, f32[256,1,8,128]{3,2,1,0:T(8,128)S(1)}, u32[]{:S(2)}, u32[]{:S(2)}) collective-permute-start(f32[256,1,8,128]{3,2,1,0:T(8,128)S(1)} %get-tuple-element.107), channel_id=1, source_target_pairs={{0,1},{1,2},{2,3},{3,4},{4,5},{5,6},{6,7},{8,9},{9,10},{10,11},{11... | collective-permute-start | bytes 3145736 | tf_op jit(solution)/shard_map/ppermute | solution.py:17
  36.1 4.6 %collective-permute-start.3 = (f32[256,1,8,128]{3,2,1,0:T(8,128)S(1)}, f32[256,1,8,128]{3,2,1,0:T(8,128)S(1)}, u32[]{:S(2)}, u32[]{:S(2)}) collective-permute-start(f32[256,1,8,128]{3,2,1,0:T(8,128)S(1)} %get-tuple-element.108), channel_id=1, source_target_pairs={{1,0},{2,1},{3,2},{4,3},{5,4},{6,5},{7,6},{9,8},{10,9},{11,10},{12... | collective-permute-start | bytes 3145736 | tf_op jit(solution)/shard_map/ppermute | solution.py:18
  47.1 182.7 %all-gather.5.cloned.1.call-start = ((), (), s32[]{:S(2)}) async-start(), calls=%async_computation.1 | async-start | bytes 9437184 | tf_op jit(solution)/shard_map/all_gather | solution.py:67
Sparse Core Ops, SparseCore 0:
  47.2 98.8 all-gather.2
  147.8 82.0 all-gather.4
where the time goes:
time: 403 us; the launch traced here: 402 us
  waiting for transfers between devices  191 us (47%)
  matrix products  147 us (36%)
  other arithmetic  21.3 us (5%)
  starting transfers between devices  19.3 us (5%)
  between operations  14.2 us (4%)
  local copies, waits for them, and re-layouts  9.25 us (2%)
    dot_general x16, matrix products, one_slice(): lax.dot_general(matrix, source, (((0,), (0,)), ((), ())), preferred_eleme...  147 us
    all_gather x1, waiting for transfers between devices, local(): everyone = lax.all_gather(flattened, 'vel', axis=0, tiled=True)  98.3 us
    all_gather x1, waiting for transfers between devices, local(): lax.all_gather(kernel_slices, 'space', axis=0, tiled=True)  83.7 us
    ppermute x2, starting transfers between devices, extended(): before = lax.ppermute(last, axis, up)  16.6 us
    mul x16, other arithmetic, one_slice(): return running + weight * projected  13.6 us
  transfers between devices with their start and end apart: 6, of which 6 were waited for; matrix products, arithmetic and copies ran while one was open for 0% of the time, Pallas kernels for 0%

commit v1 on v0

v1 whole, which is shorter than its diff:
```python
import functools

import jax
import jax.numpy as jnp
from jax import lax
from jax.experimental import pallas as pl
from jax.experimental.pallas import tpu as pltpu
from jax.sharding import PartitionSpec as P

MESH = pl.DeviceIdType.MESH
HOP_STEPS = (4, 6)


def minmod(left, right):
    small = jnp.where(left > 0, jnp.minimum(left, right), jnp.maximum(left, right))
    return jnp.where(left * right > 0, small, jnp.zeros_like(left))


def kernel(
    nv, ns, nx, ny, vl, nsl,
    dens_ref, lim_ref, vel_ref, ker_ref,
    trans_ref, coll_ref,
    acc, gath, kt, send_up, send_dn, recv_lo, recv_hi, lim_lo, lim_hi,
    halo_s, halo_r, lim_s, lim_r, v1_s, v1_r, v2_s, v2_r, k_s, k_r, c_s, c_r,
):
    vels = nv * vl
    lanes = dens_ref.shape[1]
    stride = vels // (nsl * ns)
    half = vl // 2
    v = lax.axis_index("vel")
    sp = lax.axis_index("space")
    nz = ns // 2
    z = sp // 2
    core = sp % 2
    relay = nv == 4
    if relay:
        partners = [v + 1 - 2 * (v % 2), v + 2 - 4 * ((v // 2) % 2)]
        sources = partners
    else:
        partners = [(v + p) % nv for p in range(1, nv)]
        sources = [(v + nv - p) % nv for p in range(1, nv)]
    sibling = 2 * z + 1 - core
    z_up = 2 * ((z + 1) % nz) + core
    z_dn = 2 * ((z + nz - 1) % nz) + core
    s_up = (sp + 1) % ns
    s_dn = (sp + ns - 1) % ns
    has_lo = sp > 0
    has_hi = sp < ns - 1

    barrier = pltpu.get_barrier_semaphore()
    for p in partners:
        pl.semaphore_signal(barrier, inc=1, device_id={"vel": p}, device_id_type=MESH)
    for p in (sibling, z_up, z_dn, s_up, s_dn):
        pl.semaphore_signal(barrier, inc=1, device_id={"space": p}, device_id_type=MESH)
    pl.semaphore_wait(barrier, len(partners) + 5)

    def remote(src, dst, ss, rs, axis, peer):
        return pltpu.make_async_remote_copy(
            src_ref=src, dst_ref=dst, send_sem=ss, recv_sem=rs,
            device_id={axis: peer}, device_id_type=MESH,
        )

    def halo_up(y):
        return remote(send_up.at[y], recv_lo.at[y], halo_s.at[0, y], halo_r.at[0, y], "space", s_up)

    def halo_dn(y):
        return remote(send_dn.at[y], recv_hi.at[y], halo_s.at[1, y], halo_r.at[1, y], "space", s_dn)

    lim_up = remote(lim_ref.at[pl.ds((nx - 1) * ny, ny)], lim_lo, lim_s.at[0], lim_r.at[0], "space", s_up)
    lim_dn = remote(lim_ref.at[pl.ds(0, ny)], lim_hi, lim_s.at[1], lim_r.at[1], "space", s_dn)

    @pl.when(has_hi)
    def _():
        lim_up.start()

    @pl.when(has_lo)
    def _():
        lim_dn.start()

    rows = nx * ny

    def cells(x, y, start, size):
        return dens_ref[pl.ds(start * rows + x * ny + y, size, stride=rows), :]

    @pl.loop(0, ny)
    def _(y):
        send_up[y, 0] = cells(nx - 1, y, 0, vl).astype(jnp.bfloat16)
        send_up[y, 1] = cells(nx - 2, y, 0, vl).astype(jnp.bfloat16)
        send_dn[y, 0] = cells(0, y, 0, vl).astype(jnp.bfloat16)
        send_dn[y, 1] = cells(1, y, 0, vl).astype(jnp.bfloat16)

        @pl.when(has_hi)
        def _():
            halo_up(y).start()

        @pl.when(has_lo)
        def _():
            halo_dn(y).start()

    def block(shard):
        return kt.at[pl.ds(shard * nsl, nsl)]

    blk = min(256, vels)

    @pl.loop(0, nsl)
    def _(i):
        for j in range(0, vels, blk):
            kt[sp * nsl + i, :, j : j + blk] = ker_ref[i, j : j + blk, :].T

    hops = nz // 2

    def k_piece(chip, hop, up):
        shard = 2 * chip + core
        if nz % 2 == 0 and hop == hops:
            first = 0 if up else half
            return kt.at[pl.ds(shard * nsl, nsl), pl.ds(first, half)]
        return block(shard)

    def k_hop(hop, up):
        if up:
            piece = k_piece((z + nz - (hop - 1)) % nz, hop, True)
            return remote(piece, piece, k_s.at[0, hop - 1], k_r.at[0, hop - 1], "space", z_up)
        piece = k_piece((z + hop - 1) % nz, hop, False)
        return remote(piece, piece, k_s.at[1, hop - 1], k_r.at[1, hop - 1], "space", z_dn)

    def k_arrival(hop, up):
        if up:
            piece = k_piece((z + nz - hop) % nz, hop, True)
            return remote(piece, piece, k_s.at[0, hop - 1], k_r.at[0, hop - 1], "space", z_up)
        piece = k_piece((z + hop) % nz, hop, False)
        return remote(piece, piece, k_s.at[1, hop - 1], k_r.at[1, hop - 1], "space", z_dn)

    def chip_of(n):
        if n == 0:
            return z
        d = (n + 1) // 2
        return (z + d) % nz if n % 2 else (z + nz - d) % nz

    def across(n):
        piece = block(2 * chip_of(n) + core)
        return remote(piece, piece, c_s.at[n], c_r.at[n], "space", sibling)

    def from_sibling(n):
        piece = block(2 * chip_of(n) + 1 - core)
        return remote(piece, piece, c_s.at[n], c_r.at[n], "space", sibling)

    if hops:
        k_hop(1, True).start()
        k_hop(1, False).start()
    across(0).start()

    @pl.when(has_lo)
    def _():
        lim_up.wait_recv()

    @pl.when(has_hi)
    def _():
        lim_dn.wait_recv()

    @pl.when(jnp.logical_not(has_lo))
    def _():
        lim_lo[...] = jnp.zeros_like(lim_lo)
        recv_lo[...] = jnp.zeros_like(recv_lo)

    @pl.when(jnp.logical_not(has_hi))
    def _():
        lim_hi[...] = jnp.zeros_like(lim_hi)
        recv_hi[...] = jnp.zeros_like(recv_hi)

    def slope(left, right, code):
        central = 0.5 * (left + right)
        return jnp.where(
            code == 1, minmod(left, right), jnp.where(code == 2, central, jnp.zeros_like(central))
        )

    rb = 32

    def transport(y):
        @pl.loop(0, vl // rb)
        def _(b):
            r0 = pl.multiple_of(b * rb, rb)
            signed = vel_ref[pl.ds(r0, rb), :]
            forward = signed > 0
            cour = jnp.abs(signed)
            upw = jnp.where(forward, jnp.float32(0.5), jnp.float32(-0.5))
            d = [recv_lo[y, 1, pl.ds(r0, rb), :].astype(jnp.float32),
                 recv_lo[y, 0, pl.ds(r0, rb), :].astype(jnp.float32)]
            d += [cells(x, y, r0, rb) for x in range(nx)]
            d += [recv_hi[y, 0, pl.ds(r0, rb), :].astype(jnp.float32),
                  recv_hi[y, 1, pl.ds(r0, rb), :].astype(jnp.float32)]
            codes = [lim_lo[pl.ds(y, 1), :]]
            codes += [lim_ref[pl.ds(x * ny + y, 1), :] for x in range(nx)]
            codes += [lim_hi[pl.ds(y, 1), :]]
            diff = [d[i + 1] - d[i] for i in range(nx + 3)]
            r = []
            for i in range(nx + 2):
                code = jnp.broadcast_to(codes[i], (rb, lanes))
                r.append(d[i + 1] + upw * slope(diff[i], diff[i + 1], code))
            for x in range(nx):
                upstream = jnp.where(forward, r[x], r[x + 2])
                out = d[x + 2] - cour * (r[x + 1] - upstream)
                trans_ref[pl.ds(r0 * rows + x * ny + y, rb, stride=rows), :] = out
                gath[y, pl.ds(pl.multiple_of(v * vl + r0, rb), rb), x * lanes : (x + 1) * lanes] = (
                    out.astype(jnp.bfloat16)
                )

    def mine(y, owner):
        return gath.at[y, pl.ds(pl.multiple_of(owner * vl, vl), vl)]

    def first_phase(y, p):
        return remote(mine(y, v), mine(y, v), v1_s.at[p, y], v1_r.at[p, y], "vel", partners[p])

    def first_arrival(y, p):
        piece = mine(y, sources[p])
        return remote(piece, piece, v1_s.at[p, y], v1_r.at[p, y], "vel", partners[p])

    def part(y, owner, which):
        return gath.at[y, pl.ds(pl.multiple_of(owner * vl + which * half, half), half)]

    def second_phase(y, p):
        piece = part(y, partners[1 - p], p)
        return remote(piece, piece, v2_s.at[p, y], v2_r.at[p, y], "vel", partners[p])

    def second_arrival(y, p):
        far = partners[0] + partners[1] - v
        piece = part(y, far, p)
        return remote(piece, piece, v2_s.at[p, y], v2_r.at[p, y], "vel", partners[p])

    def one(c, shard):
        total = acc[c]
        for i in range(nsl):
            s = shard * nsl + i
            prod = jnp.dot(kt[s], gath[c], preferred_element_type=jnp.float32)
            row = gath[c, pl.ds(pl.multiple_of(s * stride, stride), 1), :].astype(jnp.float32)
            total = total + row * prod
        acc[c] = total

    def shard_at(n):
        k = n // 2
        odd = k % 2
        d = (k + 1) // 2
        chip = (z + odd * d + (1 - odd) * (nz - d)) % nz
        return 2 * chip + (core + n % 2) % 2

    at_one = min(HOP_STEPS[0], ny - 1)
    at_far = min(HOP_STEPS[1], ny - 1)
    n_near = min(3, nz)

    def compute(c, first, last, start):
        early = jnp.where(c < start, c + 1, jnp.where(c == start, 0, c))

        @pl.loop(early, c + 1)
        def _(cc):
            @pl.loop(first, last)
            def _(n):
                one(cc, shard_at(n))

    acc[...] = jnp.zeros_like(acc)

    @pl.loop(0, ny + 2)
    def _(t):
        @pl.when(t < ny)
        def _():
            @pl.when(has_lo)
            def _():
                halo_up(t).wait_recv()

            @pl.when(has_hi)
            def _():
                halo_dn(t).wait_recv()

            transport(t)
            for p in range(len(partners)):
                first_phase(t, p).start()

        @pl.when(jnp.logical_and(t >= 1, t < ny + 1))
        def _():
            for p in range(len(partners)):
                first_arrival(t - 1, p).wait_recv()
            if relay:
                for p in range(2):
                    second_phase(t - 1, p).start()

        @pl.when(t == at_one + 1)
        def _():
            if hops:
                for up in (True, False):
                    k_arrival(1, up).wait_recv()
                if hops > 1:
                    for up in (True, False):
                        k_hop(2, up).start()
                for n in range(1, n_near):
                    across(n).start()

        @pl.when(t == at_far + 1)
        def _():
            for hop in range(2, hops + 1):
                for up in (True, False):
                    k_arrival(hop, up).wait_recv()
                if hop < hops:
                    for up in (True, False):
                        k_hop(hop + 1, up).start()
            for n in range(n_near, nz):
                across(n).start()

        @pl.when(t == 2)
        def _():
            from_sibling(0).wait_recv()

        @pl.when(t >= 2)
        def _():
            c = t - 2
            if relay:
                for p in range(2):
                    second_arrival(c, p).wait_recv()
            compute(c, 0, 2, 0)

            @pl.when(c == at_one)
            def _():
                for n in range(1, n_near):
                    from_sibling(n).wait_recv()

            compute(c, 2, 2 * n_near, at_one)

            @pl.when(c == at_far)
            def _():
                for n in range(n_near, nz):
                    from_sibling(n).wait_recv()

            compute(c, 2 * n_near, ns, at_far)

    @pl.loop(0, ny)
    def _(y):
        for x in range(nx):
            coll_ref[pl.ds(x * ny + y, vl, stride=rows), :] = acc[y, :, x * lanes : (x + 1) * lanes]

        @pl.when(has_hi)
        def _():
            halo_up(y).wait_send()

        @pl.when(has_lo)
        def _():
            halo_dn(y).wait_send()

        for p in range(len(partners)):
            first_phase(y, p).wait_send()
        if relay:
            for p in range(2):
                second_phase(y, p).wait_send()

    @pl.when(has_hi)
    def _():
        lim_up.wait_send()

    @pl.when(has_lo)
    def _():
        lim_dn.wait_send()

    for hop in range(1, hops + 1):
        for up in (True, False):
            k_hop(hop, up).wait_send()
    for n in range(nz):
        across(n).wait_send()


def local(nv, ns, density, limiter, heading, courant, kernel_slices):
    vl, nx, ny, lanes = density.shape
    nsl, vels, _ = kernel_slices.shape
    rows = nx * ny
    nz = ns // 2
    bf16, f32 = jnp.bfloat16, jnp.float32
    dens = density.reshape(vl * rows, lanes)
    lim = limiter.reshape(rows, lanes)
    signed = jnp.where(heading == 1, courant, -courant)
    signed = jnp.broadcast_to(signed[:, None], (vl, lanes))
    dma = pltpu.SemaphoreType.DMA
    n_part = 2 if nv == 4 else max(nv - 1, 1)
    vmem = pl.BlockSpec(memory_space=pltpu.VMEM)
    out = jax.ShapeDtypeStruct(dens.shape, f32)
    hops = max(nz // 2, 1)
    trans, coll = pl.pallas_call(
        functools.partial(kernel, nv, ns, nx, ny, vl, nsl),
        out_shape=(out, out),
        in_specs=[vmem] * 4,
        out_specs=(vmem, vmem),
        scratch_shapes=[
            pltpu.VMEM((ny, vl, nx * lanes), f32),
            pltpu.VMEM((ny, vels, nx * lanes), bf16),
            pltpu.VMEM((nsl * ns, vl, vels), bf16),
            pltpu.VMEM((ny, 2, vl, lanes), bf16),
            pltpu.VMEM((ny, 2, vl, lanes), bf16),
            pltpu.VMEM((ny, 2, vl, lanes), bf16),
            pltpu.VMEM((ny, 2, vl, lanes), bf16),
            pltpu.VMEM((ny, lanes), jnp.int32),
            pltpu.VMEM((ny, lanes), jnp.int32),
            dma((2, ny)), dma((2, ny)), dma((2,)), dma((2,)),
            dma((n_part, ny)), dma((n_part, ny)), dma((2, ny)), dma((2, ny)),
            dma((2, hops)), dma((2, hops)), dma((nz,)), dma((nz,)),
        ],
        compiler_params=pltpu.CompilerParams(
            collective_id=0, has_side_effects=True, vmem_limit_bytes=60 * 1024 * 1024
        ),
    )(dens, lim, signed, kernel_slices)
    return trans.reshape(density.shape), coll.reshape(density.shape)


def solution(mesh):
    return jax.shard_map(
        functools.partial(local, mesh.shape["vel"], mesh.shape["space"]),
        mesh=mesh,
        in_specs=(
            P("vel", "space", None, None),
            P("space", None, None),
            P("vel"),
            P("vel"),
            P("space", None, "vel"),
        ),
        out_specs=(P("vel", "space", None, None), P("vel", "space", None, None)),
        check_vma=False,
    )
```

time: 403 us -> 151 us (0.37)
  waiting for transfers between devices: 191 us -> 0 us
  matrix products: 147 us -> 0 us
  Pallas kernels: 0 us -> 142 us
  other arithmetic: 21.3 us -> 0.7 us
  starting transfers between devices: 19.3 us -> 0 us
  between operations: 14.2 us -> 0.65 us
    all_gather x2 -> x0, waiting for transfers between devices: 182 us -> none  [the longest x1 98.3 us: local(): everyone = lax.all_gather(flattened, 'vel', axis=0, tiled=True)]
    dot_general x16 -> x0, matrix products: 147 us -> none  [one_slice(): lax.dot_general(matrix, source, (((0,), (0,)), ((), ())), preferred_eleme...]
    pallas_call x0 -> x1, Pallas kernels: none -> 142 us  [local(): pl.pallas_call(functools.partial(kernel, nv, ns, nx, ny, vl, nsl), out_sh...]
    ppermute x4 -> x0, starting transfers between devices: 19.2 us -> none  [the longest x2 16.6 us: extended(): before = lax.ppermute(last, axis, up)]
    mul x17 -> x0, other arithmetic: 13.6 us -> none  [the longest x16 13.6 us: one_slice(): return running + weight * projected]
    ppermute x4 -> x0, waiting for transfers between devices: 8.56 us -> none  [the longest x2 6.82 us: extended(): after = lax.ppermute(first, axis, down)]
    convert_element_type x1 -> x0, other arithmetic: 4.11 us -> none  [local(): flattened = transported.astype(jnp.bfloat16).reshape(density.shape[0], -1)]
  transfers between devices with their start and end apart: 6 -> 0, of which waited for: 6 -> 0; matrix products, arithmetic and copies ran while one was open for 0% -> 0% of each run, Pallas kernels for 0% -> 0%
where the time goes in v1:
time: 151 us; the launch traced here: 150 us
  Pallas kernels  142 us (94%)
  local copies, waits for them, and re-layouts  7.59 us (5%)
    pallas_call x1, Pallas kernels, local(): pl.pallas_call(functools.partial(kernel, nv, ns, nx, ny, vl, nsl), out_sh...  142 us
    unnamed x4, local copies, waits for them, and re-layouts  6.84 us

profile of v1, /device:TPU:0, one launch (start us, length us, event | category | flops | bytes accessed | tf_op | source)
XLA Modules:
  0.0 150.5 jit_solution(16507747169029963177)
XLA Ops:
  0.6 0.7 compare_select_fusion
  1.3 0.8 broadcast_in_dim.2.vel_ref
  2.1 141.5 %shard_map.68 = (f32[8192,128]{1,0:T(8,128)}, f32[8192,128]{1,0:T(8,128)}) custom-call(f32[8192,128]{1,0:T(8,128)} %bitcast.4, s32[32,128]{1,0:T(8,128)} %bitcast.7, f32[256,128]{1,0:T(8,128)} %broadcast_in_dim.2.vel_ref, bf16[2,1024,256]{2,1,0:T(8,128)(2,1)} %ker_ref.1), custom_call_target="tpu_custom_call" | custom-call | tf_op jit(solution)/shard_map/pallas_call | solution.py:381
  143.6 0.0 copy-start
  143.6 4.8 %copy.9 = f32[256,4,8,128]{3,2,1,0:T(8,128)} copy(f32[256,4,8,128]{3,2,1,0:T(8,128)} %bitcast.6) | data formatting | bytes 8388608
  148.5 0.0 copy-done
  148.5 2.0 %copy.10 = f32[256,4,8,128]{3,2,1,0:T(8,128)} copy(f32[256,4,8,128]{3,2,1,0:T(8,128)S(1)} %bitcast.5) | data formatting | bytes 8388608
Async XLA Ops:
  143.6 4.8 %copy-start = (f32[8192,128]{1,0:T(8,128)S(1)}, f32[8192,128]{1,0:T(8,128)}, u32[]{:S(2)}) copy-start(f32[8192,128]{1,0:T(8,128)} %get-tuple-element.5) | copy-start | bytes 12582916

commit v2 on v1

v2 whole, which is shorter than its diff:
```python
import functools

import jax
import jax.numpy as jnp
from jax import lax
from jax.experimental import pallas as pl
from jax.experimental.pallas import tpu as pltpu
from jax.sharding import PartitionSpec as P

MESH = pl.DeviceIdType.MESH


def minmod(left, right):
    small = jnp.where(left > 0, jnp.minimum(left, right), jnp.maximum(left, right))
    return jnp.where(left * right > 0, small, jnp.zeros_like(left))


def kernel(
    nv, ns, nx, ny, vl, nsl,
    dens_ref, lim_ref, vel_ref, ker_ref,
    trans_ref, coll_ref,
    acc, gath, kt, send_up, send_dn, recv_lo, recv_hi, lim_lo, lim_hi,
    dbuf, in_s, trans_s, coll_s,
    halo_s, halo_r, lim_s, lim_r, v1_s, v1_r, v2_s, v2_r, k_s, k_r, c_s, c_r,
):
    vels = nv * vl
    lanes = dens_ref.shape[3]
    stride = vels // (nsl * ns)
    half = vl // 2
    v = lax.axis_index("vel")
    sp = lax.axis_index("space")
    nz = ns // 2
    z = sp // 2
    core = sp % 2
    relay = nv == 4
    if relay:
        partners = [v + 1 - 2 * (v % 2), v + 2 - 4 * ((v // 2) % 2)]
        sources = partners
    else:
        partners = [(v + p) % nv for p in range(1, nv)]
        sources = [(v + nv - p) % nv for p in range(1, nv)]
    sibling = 2 * z + 1 - core
    z_up = 2 * ((z + 1) % nz) + core
    z_dn = 2 * ((z + nz - 1) % nz) + core
    s_up = (sp + 1) % ns
    s_dn = (sp + ns - 1) % ns
    has_lo = sp > 0
    has_hi = sp < ns - 1
    groups = nz * nsl

    def load(x, y):
        return pltpu.make_async_copy(dens_ref.at[:, x * ny + y, 0, :], dbuf.at[y, x], in_s.at[y, x])

    def save(x, y):
        return pltpu.make_async_copy(dbuf.at[y, x], trans_ref.at[:, x * ny + y, 0, :], trans_s.at[y, x])

    def give(x, y):
        tile = acc.at[y, :, pl.ds(x * lanes, lanes)]
        return pltpu.make_async_copy(tile, coll_ref.at[:, x * ny + y, 0, :], coll_s.at[y, x])

    @pl.loop(0, ny)
    def _(y):
        for x in range(nx):
            load(x, y).start()

    barrier = pltpu.get_barrier_semaphore()
    for p in partners:
        pl.semaphore_signal(barrier, inc=1, device_id={"vel": p}, device_id_type=MESH)
    for p in (sibling, z_up, z_dn, s_up, s_dn):
        pl.semaphore_signal(barrier, inc=1, device_id={"space": p}, device_id_type=MESH)
    pl.semaphore_wait(barrier, len(partners) + 5)

    def remote(src, dst, ss, rs, axis, peer):
        return pltpu.make_async_remote_copy(
            src_ref=src, dst_ref=dst, send_sem=ss, recv_sem=rs,
            device_id={axis: peer}, device_id_type=MESH,
        )

    def halo_up(y):
        return remote(send_up.at[y], recv_lo.at[y], halo_s.at[0, y], halo_r.at[0, y], "space", s_up)

    def halo_dn(y):
        return remote(send_dn.at[y], recv_hi.at[y], halo_s.at[1, y], halo_r.at[1, y], "space", s_dn)

    lim_up = remote(lim_ref.at[pl.ds((nx - 1) * ny, ny)], lim_lo, lim_s.at[0], lim_r.at[0], "space", s_up)
    lim_dn = remote(lim_ref.at[pl.ds(0, ny)], lim_hi, lim_s.at[1], lim_r.at[1], "space", s_dn)

    @pl.when(has_hi)
    def _():
        lim_up.start()

    @pl.when(has_lo)
    def _():
        lim_dn.start()

    blk = min(256, vels)

    def chip_at(way, h):
        return z - h if way == 0 else z + h

    def held(way, h):
        return z - h >= 0 if way == 0 else z + h < nz

    def slice_of(way, h, i, c):
        return kt.at[pl.ds((2 * chip_at(way, h) + c) * nsl + i, 1)]

    def onward(way, h, i):
        piece = slice_of(way, h, i, core)
        return remote(piece, piece, k_s.at[way, h, i], k_r.at[way, h, i], "space", (z_up, z_dn)[way])

    def sends(way, h):
        more = z < nz - 1 if way == 0 else z > 0
        return jnp.logical_and(more, held(way, h))

    def arrival(way, h, i):
        piece = slice_of(way, h, i, core)
        return remote(piece, piece, k_s.at[way, h - 1, i], k_r.at[way, h - 1, i], "space", (z_up, z_dn)[way])

    def across(way, h, i):
        piece = slice_of(way, h, i, core)
        return remote(piece, piece, c_s.at[way, h, i], c_r.at[way, h, i], "space", sibling)

    def from_sibling(way, h, i):
        piece = slice_of(way, h, i, 1 - core)
        return remote(piece, piece, c_s.at[way, h, i], c_r.at[way, h, i], "space", sibling)

    @pl.loop(0, nsl)
    def _(i):
        for j in range(0, vels, blk):
            kt[sp * nsl + i, :, j : j + blk] = ker_ref[i, j : j + blk, :].T
        for way in range(2):
            @pl.when(sends(way, 0))
            def _():
                onward(way, 0, i).start()
        across(0, 0, i).start()

    @pl.loop(0, ny)
    def _(y):
        for x in range(nx):
            load(x, y).wait()
        send_up[y, 0] = dbuf[y, nx - 1].astype(jnp.bfloat16)
        send_up[y, 1] = dbuf[y, nx - 2].astype(jnp.bfloat16)
        send_dn[y, 0] = dbuf[y, 0].astype(jnp.bfloat16)
        send_dn[y, 1] = dbuf[y, 1].astype(jnp.bfloat16)

        @pl.when(has_hi)
        def _():
            halo_up(y).start()

        @pl.when(has_lo)
        def _():
            halo_dn(y).start()

    @pl.when(has_lo)
    def _():
        lim_up.wait_recv()

    @pl.when(has_hi)
    def _():
        lim_dn.wait_recv()

    @pl.when(jnp.logical_not(has_lo))
    def _():
        lim_lo[...] = jnp.zeros_like(lim_lo)
        recv_lo[...] = jnp.zeros_like(recv_lo)

    @pl.when(jnp.logical_not(has_hi))
    def _():
        lim_hi[...] = jnp.zeros_like(lim_hi)
        recv_hi[...] = jnp.zeros_like(recv_hi)

    def slope(left, right, code):
        central = 0.5 * (left + right)
        return jnp.where(
            code == 1, minmod(left, right), jnp.where(code == 2, central, jnp.zeros_like(central))
        )

    rb = 32

    def transport(y):
        @pl.loop(0, vl // rb)
        def _(b):
            r0 = pl.multiple_of(b * rb, rb)
            signed = vel_ref[pl.ds(r0, rb), :]
            forward = signed > 0
            cour = jnp.abs(signed)
            upw = jnp.where(forward, jnp.float32(0.5), jnp.float32(-0.5))
            d = [recv_lo[y, 1, pl.ds(r0, rb), :].astype(jnp.float32),
                 recv_lo[y, 0, pl.ds(r0, rb), :].astype(jnp.float32)]
            d += [dbuf[y, x, pl.ds(r0, rb), :] for x in range(nx)]
            d += [recv_hi[y, 0, pl.ds(r0, rb), :].astype(jnp.float32),
                  recv_hi[y, 1, pl.ds(r0, rb), :].astype(jnp.float32)]
            codes = [lim_lo[pl.ds(y, 1), :]]
            codes += [lim_ref[pl.ds(x * ny + y, 1), :] for x in range(nx)]
            codes += [lim_hi[pl.ds(y, 1), :]]
            diff = [d[i + 1] - d[i] for i in range(nx + 3)]
            r = []
            for i in range(nx + 2):
                code = jnp.broadcast_to(codes[i], (rb, lanes))
                r.append(d[i + 1] + upw * slope(diff[i], diff[i + 1], code))
            for x in range(nx):
                upstream = jnp.where(forward, r[x], r[x + 2])
                out = d[x + 2] - cour * (r[x + 1] - upstream)
                dbuf[y, x, pl.ds(r0, rb), :] = out
                gath[y, pl.ds(pl.multiple_of(v * vl + r0, rb), rb), x * lanes : (x + 1) * lanes] = (
                    out.astype(jnp.bfloat16)
                )

    def mine(y, owner):
        return gath.at[y, pl.ds(pl.multiple_of(owner * vl, vl), vl)]

    def first_phase(y, p):
        return remote(mine(y, v), mine(y, v), v1_s.at[p, y], v1_r.at[p, y], "vel", partners[p])

    def first_arrival(y, p):
        piece = mine(y, sources[p])
        return remote(piece, piece, v1_s.at[p, y], v1_r.at[p, y], "vel", partners[p])

    def part(y, owner, which):
        return gath.at[y, pl.ds(pl.multiple_of(owner * vl + which * half, half), half)]

    def second_phase(y, p):
        piece = part(y, partners[1 - p], p)
        return remote(piece, piece, v2_s.at[p, y], v2_r.at[p, y], "vel", partners[p])

    def second_arrival(y, p):
        far = partners[0] + partners[1] - v
        piece = part(y, far, p)
        return remote(piece, piece, v2_s.at[p, y], v2_r.at[p, y], "vel", partners[p])

    def one(c, chip, i):
        total = acc[c]
        for k in range(2):
            s = (2 * chip + k) * nsl + i
            prod = jnp.dot(kt[s], gath[c], preferred_element_type=jnp.float32)
            row = gath[c, pl.ds(pl.multiple_of(s * stride, stride), 1), :].astype(jnp.float32)
            total = total + row * prod
        acc[c] = total

    def first_chunk(g):
        later = jnp.clip(((g - 1) * ny) // groups, 1, ny - 1)
        return jnp.where(g < nsl, 0, later)

    def compute(c):
        @pl.loop(0, groups)
        def _(g):
            h, i = g // nsl, g % nsl
            start = first_chunk(g)
            early = jnp.where(c < start, c + 1, jnp.where(c == start, 0, c))
            for way in range(2):
                here = held(way, h) if way == 0 else jnp.logical_and(h > 0, held(way, h))

                @pl.when(jnp.logical_and(here, c == start))
                def _():
                    from_sibling(way, h, i).wait_recv()

            @pl.loop(early, c + 1)
            def _(cc):
                low = jnp.where(z - h >= 0, 0, 1)
                high = jnp.where(jnp.logical_and(h > 0, z + h < nz), 2, 1)

                @pl.loop(low, high)
                def _(way):
                    one(cc, z + (2 * way - 1) * h, i)

                @pl.when(jnp.logical_and(g == groups - 1, c >= start))
                def _():
                    for x in range(nx):
                        give(x, cc).start()

    def service(c):
        @pl.loop(nsl, groups)
        def _(g):
            h, i = g // nsl, g % nsl

            @pl.when(first_chunk(g) == c)
            def _():
                for way in range(2):
                    @pl.when(held(way, h))
                    def _():
                        arrival(way, h, i).wait_recv()

                        @pl.when(sends(way, h))
                        def _():
                            onward(way, h, i).start()

                        across(way, h, i).start()

    @pl.loop(0, ny + 2)
    def _(t):
        @pl.when(t < ny)
        def _():
            @pl.when(has_lo)
            def _():
                halo_up(t).wait_recv()

            @pl.when(has_hi)
            def _():
                halo_dn(t).wait_recv()

            transport(t)
            for p in range(len(partners)):
                first_phase(t, p).start()
            for x in range(nx):
                save(x, t).start()

        @pl.when(jnp.logical_and(t >= 1, t < ny + 1))
        def _():
            for p in range(len(partners)):
                first_arrival(t - 1, p).wait_recv()
            if relay:
                for p in range(2):
                    second_phase(t - 1, p).start()

        @pl.when(t >= 2)
        def _():
            c = t - 2
            if relay:
                for p in range(2):
                    second_arrival(c, p).wait_recv()
            acc[c] = jnp.zeros_like(acc[c])
            compute(c)
            service(c + 1)

    @pl.loop(0, ny)
    def _(y):
        for x in range(nx):
            save(x, y).wait()
            give(x, y).wait()

        @pl.when(has_hi)
        def _():
            halo_up(y).wait_send()

        @pl.when(has_lo)
        def _():
            halo_dn(y).wait_send()

        for p in range(len(partners)):
            first_phase(y, p).wait_send()
        if relay:
            for p in range(2):
                second_phase(y, p).wait_send()

    @pl.when(has_hi)
    def _():
        lim_up.wait_send()

    @pl.when(has_lo)
    def _():
        lim_dn.wait_send()

    @pl.loop(0, groups)
    def _(g):
        h, i = g // nsl, g % nsl
        for way in range(2):
            @pl.when(sends(way, h))
            def _():
                onward(way, h, i).wait_send()

            here = held(way, h) if way == 0 else jnp.logical_and(h > 0, held(way, h))

            @pl.when(here)
            def _():
                across(way, h, i).wait_send()


def local(nv, ns, density, limiter, heading, courant, kernel_slices):
    vl, nx, ny, lanes = density.shape
    nsl, vels, _ = kernel_slices.shape
    rows = nx * ny
    nz = ns // 2
    bf16, f32 = jnp.bfloat16, jnp.float32
    dens = density.reshape(vl, rows, 1, lanes)
    lim = limiter.reshape(rows, lanes)
    signed = jnp.where(heading == 1, courant, -courant)
    signed = jnp.broadcast_to(signed[:, None], (vl, lanes))
    dma = pltpu.SemaphoreType.DMA
    n_part = 2 if nv == 4 else max(nv - 1, 1)
    vmem = pl.BlockSpec(memory_space=pltpu.VMEM)
    out = jax.ShapeDtypeStruct(dens.shape, f32)
    hbm = pl.BlockSpec(memory_space=pl.ANY)
    trans, coll = pl.pallas_call(
        functools.partial(kernel, nv, ns, nx, ny, vl, nsl),
        out_shape=(out, out),
        in_specs=[hbm, vmem, vmem, vmem],
        out_specs=(hbm, hbm),
        scratch_shapes=[
            pltpu.VMEM((ny, vl, nx * lanes), f32),
            pltpu.VMEM((ny, vels, nx * lanes), bf16),
            pltpu.VMEM((nsl * ns, vl, vels), bf16),
            pltpu.VMEM((ny, 2, vl, lanes), bf16),
            pltpu.VMEM((ny, 2, vl, lanes), bf16),
            pltpu.VMEM((ny, 2, vl, lanes), bf16),
            pltpu.VMEM((ny, 2, vl, lanes), bf16),
            pltpu.VMEM((ny, lanes), jnp.int32),
            pltpu.VMEM((ny, lanes), jnp.int32),
            pltpu.VMEM((ny, nx, vl, lanes), f32),
            dma((ny, nx)), dma((ny, nx)), dma((ny, nx)),
            dma((2, ny)), dma((2, ny)), dma((2,)), dma((2,)),
            dma((n_part, ny)), dma((n_part, ny)), dma((2, ny)), dma((2, ny)),
            dma((2, nz, nsl)), dma((2, nz, nsl)), dma((2, nz, nsl)), dma((2, nz, nsl)),
        ],
        compiler_params=pltpu.CompilerParams(
            collective_id=0, has_side_effects=True, vmem_limit_bytes=60 * 1024 * 1024
        ),
    )(dens, lim, signed, kernel_slices)
    return trans.reshape(density.shape), coll.reshape(density.shape)


def solution(mesh):
    return jax.shard_map(
        functools.partial(local, mesh.shape["vel"], mesh.shape["space"]),
        mesh=mesh,
        in_specs=(
            P("vel", "space", None, None),
            P("space", None, None),
            P("vel"),
            P("vel"),
            P("space", None, "vel"),
        ),
        out_specs=(P("vel", "space", None, None), P("vel", "space", None, None)),
        check_vma=False,
    )
```

time: 151 us -> 128 us (0.85)
  Pallas kernels: 142 us -> 119 us
    pallas_call x1, Pallas kernels: 142 us -> 119 us  [local(): pl.pallas_call(functools.partial(kernel, nv, ns, nx, ny, vl, nsl), out_sh...]
where the time goes in v2:
time: 128 us
  Pallas kernels  119 us (93%)
  local copies, waits for them, and re-layouts  7.59 us (6%)
    pallas_call x1, Pallas kernels, local(): pl.pallas_call(functools.partial(kernel, nv, ns, nx, ny, vl, nsl), out_sh...  119 us
    unnamed x4, local copies, waits for them, and re-layouts  6.84 us

profile of v2, /device:TPU:0, one launch (start us, length us, event | category | flops | bytes accessed | tf_op | source)
XLA Modules:
  0.0 127.5 jit_solution(4980761773762474878)
XLA Ops:
  0.6 0.7 compare_select_fusion
  1.3 0.8 broadcast_in_dim.2.vel_ref
  2.1 118.6 %shard_map.68 = (f32[256,32,1,128]{3,2,1,0:T(1,128)}, f32[256,32,1,128]{3,2,1,0:T(1,128)}) custom-call(f32[256,32,1,128]{3,2,1,0:T(1,128)} %bitcast.4, s32[32,128]{1,0:T(8,128)} %bitcast.7, f32[256,128]{1,0:T(8,128)} %broadcast_in_dim.2.vel_ref, bf16[2,1024,256]{2,1,0:T(8,128)(2,1)} %ker_ref.1), custom_call_target="tpu_custom_call" | custom-call | tf_op jit(solution)/shard_map/pallas_call | solution.py:383
  120.7 0.0 copy-start
  120.7 4.8 %copy.9 = f32[256,4,8,128]{3,2,1,0:T(8,128)} copy(f32[256,4,8,128]{3,2,1,0:T(8,128)} %bitcast.6) | data formatting | bytes 8388608
  125.5 0.0 copy-done
  125.5 2.0 %copy.10 = f32[256,4,8,128]{3,2,1,0:T(8,128)} copy(f32[256,4,8,128]{3,2,1,0:T(8,128)S(1)} %bitcast.5) | data formatting | bytes 8388608
Async XLA Ops:
  120.7 4.8 %copy-start = (f32[256,32,1,128]{3,2,1,0:T(1,128)S(1)}, f32[256,32,1,128]{3,2,1,0:T(1,128)}, u32[]{:S(2)}) copy-start(f32[256,32,1,128]{3,2,1,0:T(1,128)} %get-tuple-element.5) | copy-start | bytes 12582916

commit v3 on v2

--- a/solution.py
+++ b/solution.py
@@ -128,11 +128,6 @@
     def _(i):
         for j in range(0, vels, blk):
             kt[sp * nsl + i, :, j : j + blk] = ker_ref[i, j : j + blk, :].T
-        for way in range(2):
-            @pl.when(sends(way, 0))
-            def _():
-                onward(way, 0, i).start()
-        across(0, 0, i).start()
 
     @pl.loop(0, ny)
     def _(y):
@@ -150,6 +145,14 @@
         @pl.when(has_lo)
         def _():
             halo_dn(y).start()
+
+    @pl.loop(0, nsl)
+    def _(i):
+        for way in range(2):
+            @pl.when(sends(way, 0))
+            def _():
+                onward(way, 0, i).start()
+        across(0, 0, i).start()
 
     @pl.when(has_lo)
     def _():
@@ -238,7 +241,7 @@
         acc[c] = total
 
     def first_chunk(g):
-        later = jnp.clip(((g - 1) * ny) // groups, 1, ny - 1)
+        later = jnp.clip((g * ny) // groups, 1, ny - 1)
         return jnp.where(g < nsl, 0, later)
 
     def compute(c):

time: 128 us -> 111 us (0.87)
  Pallas kernels: 119 us -> 100 us
    pallas_call x1, Pallas kernels: 119 us -> 100 us  [local(): pl.pallas_call(functools.partial(kernel, nv, ns, nx, ny, vl, nsl), out_sh...]
where the time goes in v3:
time: 111 us; the launch traced here: 109 us
  Pallas kernels  100 us (90%)
  local copies, waits for them, and re-layouts  7.59 us (7%)
    pallas_call x1, Pallas kernels, local(): pl.pallas_call(functools.partial(kernel, nv, ns, nx, ny, vl, nsl), out_sh...  100 us
    unnamed x4, local copies, waits for them, and re-layouts  6.84 us

profile of v3, /device:TPU:0, one launch (start us, length us, event | category | flops | bytes accessed | tf_op | source)
XLA Modules:
  0.0 109.4 jit_solution(455075877208958382)
XLA Ops:
  0.6 0.7 compare_select_fusion
  1.3 0.8 broadcast_in_dim.2.vel_ref
  2.1 100.5 %shard_map.68 = (f32[256,32,1,128]{3,2,1,0:T(1,128)}, f32[256,32,1,128]{3,2,1,0:T(1,128)}) custom-call(f32[256,32,1,128]{3,2,1,0:T(1,128)} %bitcast.4, s32[32,128]{1,0:T(8,128)} %bitcast.7, f32[256,128]{1,0:T(8,128)} %broadcast_in_dim.2.vel_ref, bf16[2,1024,256]{2,1,0:T(8,128)(2,1)} %ker_ref.1), custom_call_target="tpu_custom_call" | custom-call | tf_op jit(solution)/shard_map/pallas_call | solution.py:386
  102.6 0.0 copy-start
  102.6 4.8 %copy.9 = f32[256,4,8,128]{3,2,1,0:T(8,128)} copy(f32[256,4,8,128]{3,2,1,0:T(8,128)} %bitcast.6) | data formatting | bytes 8388608
  107.4 0.0 copy-done
  107.4 2.0 %copy.10 = f32[256,4,8,128]{3,2,1,0:T(8,128)} copy(f32[256,4,8,128]{3,2,1,0:T(8,128)S(1)} %bitcast.5) | data formatting | bytes 8388608
Async XLA Ops:
  102.6 4.8 %copy-start = (f32[256,32,1,128]{3,2,1,0:T(1,128)S(1)}, f32[256,32,1,128]{3,2,1,0:T(1,128)}, u32[]{:S(2)}) copy-start(f32[256,32,1,128]{3,2,1,0:T(1,128)} %get-tuple-element.5) | copy-start | bytes 12582916
